TPU v7x, 128 devices: a whole 4x4x4 slice. The times are simulated.
128 devices in a mesh: member: 16 (over z_lo, y, core), band: 8 (over x, z_hi).
Axes of the slice: x: 4, y: 4, z: 4 (z_hi: 2, z_lo: 2; z = z_hi * 2 + z_lo), core: 2. Of those that a mesh axis runs over, the one named last changes fastest.
Arguments:
- height_start: float32 [80, 512, 1024], P(None, 'member', 'band'), may hold values from -6 to 6
- east_start: float32 [80, 512, 1024], P(None, 'member', 'band'), may hold values from -6 to 6
- north_start: float32 [80, 512, 1024], P(None, 'member', 'band'), may hold values from -6 to 6
- obs_value: float32 [512, 1024], P('member', 'band'), may hold values from -8 to 8
- obs_mask: int32 [512, 1024], P('member', 'band'), may hold values 0 or 1
- obs_precision: float32 [512, 1024], P('member', 'band'), may hold values from 0.25 to 4
- step_sizes: int32 [2], replicated, may hold values from 4 to 12
Outputs:
- analysis_height: float32 [80, 512, 1024], P(None, 'member', 'band')
- analysis_east: float32 [80, 512, 1024], P(None, 'member', 'band')
- analysis_north: float32 [80, 512, 1024], P(None, 'member', 'band')
All inputs are finite; a program needn't handle non-finite values. No bound on the sum of `obs_mask` on one device may be relied on, other than what follows from the above.
Results may differ from a plain program's by a relative error of at most 0.0001.
Values sent between devices are 32-bit elements; how exact they have to be, the bound alone decides.
A program may use at most 128 MiB of HBM per device.

v0:
```python
import jax
import jax.numpy as jnp
from jax import lax
from jax.sharding import Mesh
from jax.sharding import PartitionSpec as P

STEPS = 3
ITERS = 2
LWIDTH = 32
LSCALE = 12
MEMBER = ("member_0", "member_1", "member_2")
BAND = ("band_0", "band_1")
MEMBER_BAND = ("member_0", "member_1", "member_2", "band_0", "band_1")
highest = lax.Precision.HIGHEST


def extended(block, sides, width, periodic):
    for axis, dim in sides:
        count = lax.axis_size(axis)
        forward = [(i, i + 1) for i in range(count - 1)]
        if periodic:
            forward.append((count - 1, 0))
        backward = [(target, source) for source, target in forward]
        low = lax.ppermute(
            lax.slice_in_dim(block, block.shape[dim] - width, None, axis=dim), axis, forward
        )
        high = lax.ppermute(lax.slice_in_dim(block, 0, width, axis=dim), axis, backward)
        block = jnp.concatenate([low, block, high], axis=dim)
    return block


def one_axis_at_a_time(array, axes):
    for axis in axes:
        array = lax.psum(array, axis)
    return array


def taper_kernel(outputs, inputs, margin, spread):
    out_index = jnp.arange(outputs, dtype=jnp.int32)[:, None]
    in_index = jnp.arange(inputs, dtype=jnp.int32)[None, :]
    offset = (in_index - margin - out_index).astype(jnp.float32)
    scaled_off = offset / spread
    weight = jnp.exp(-0.5 * scaled_off * scaled_off)
    return jnp.where(jnp.abs(offset) <= margin, weight, jnp.zeros_like(weight))


def taper_rows(padded, row_count, margin, spread):
    kernel = taper_kernel(row_count, row_count + 2 * margin, margin, spread)
    return jnp.einsum("ab,mbc->mac", kernel, padded, precision=highest)


def taper_columns(padded, columns, margin, spread):
    block_size = 128
    windows = jnp.stack([padded], axis=2)
    kernel = taper_kernel(block_size, block_size + 2 * margin, margin, spread)
    result = jnp.einsum("mrjk,bk->mrjb", windows, kernel, precision=highest)
    return result.reshape(padded.shape[0], padded.shape[1], columns)


def wave_edges(stacked, margin):
    rows_done = extended(stacked, ((MEMBER, 2),), margin, False)
    return extended(rows_done, ((BAND, 3),), margin, True)


def advance_deep(height, eastward, northward, valid_rows):
    padded = wave_edges(jnp.stack([height, eastward, northward]), 2)
    height_pad = padded[0]
    east_pad = padded[1]
    north_pad = padded[2]
    wide_height = height_pad[:, 1:-1, 1:-1] - 0.2 * (
        east_pad[:, 1:-1, 2:]
        - east_pad[:, 1:-1, :-2]
        + (north_pad[:, 2:, 1:-1] - north_pad[:, :-2, 1:-1])
    )
    wide_height = jnp.where(valid_rows[None, :, None], wide_height, jnp.zeros_like(wide_height))
    new_height = wide_height[:, 1:-1, 1:-1]
    new_east = (
        eastward + 0.1 * northward - 0.2 * (wide_height[:, 1:-1, 2:] - wide_height[:, 1:-1, :-2])
    )
    new_north = (
        northward - 0.1 * eastward - 0.2 * (wide_height[:, 2:, 1:-1] - wide_height[:, :-2, 1:-1])
    )
    return (new_height, new_east, new_north)


def descend(anomalies, member_means, observed, step_sizes, cell_total, gather_state, localize):
    weights = jnp.zeros_like(anomalies[0])
    for iteration in range(ITERS):
        if iteration == 0:
            analysis_state = member_means
        else:
            analysis_state = member_means + gather_state(jnp.sum(anomalies * weights[None], axis=1))
        residual = observed[1] * (
            observed[0]
            - analysis_state[0]
            - 0.15 * (analysis_state[1] * analysis_state[1] + analysis_state[2] * analysis_state[2])
        )
        contrib = (
            anomalies[0]
            + 0.3 * (analysis_state[1] * anomalies[1] + analysis_state[2] * anomalies[2])
        ) * residual
        gradient = weights - localize(contrib)
        square_total = one_axis_at_a_time(jnp.sum(gradient * gradient), MEMBER_BAND)
        factor = (
            step_sizes[iteration].astype(jnp.float32)
            / 64.0
            / jnp.sqrt(square_total / cell_total + 1e-06)
        )
        weights = weights - factor * gradient
    return weights


def analyse_tiles(ensemble, observed, step_sizes, cell_total, root_scale, members):
    member_means = jnp.sum(ensemble, axis=1) / members
    anomalies = (ensemble - member_means[:, None]) / root_scale

    def local_state(partial_sum):
        return partial_sum

    def localize(contrib):
        padded = extended(contrib, ((MEMBER, 1),), LWIDTH, False)
        lat_done = taper_rows(padded, contrib.shape[1], LWIDTH, LSCALE)
        wrapped = extended(lat_done, ((BAND, 2),), LWIDTH, True)
        return taper_columns(wrapped, contrib.shape[2], LWIDTH, LSCALE)

    weights = descend(
        anomalies, member_means, observed, step_sizes, cell_total, local_state, localize
    )
    return jnp.sum(anomalies * weights[None], axis=1)


def per_device(
    height_start, east_start, north_start, obs_value, obs_mask, obs_precision, step_sizes
):
    members = height_start.shape[0]
    row_count = height_start.shape[1]
    col_count = height_start.shape[2]
    height, eastward, northward = (height_start, east_start, north_start)
    global_rows = (
        lax.axis_index(MEMBER) * row_count - 1 + jnp.arange(row_count + 2, dtype=jnp.int32)
    )
    valid_rows = (global_rows >= 0) & (global_rows < row_count * lax.axis_size(MEMBER))
    for section_number in range(STEPS):
        height, eastward, northward = advance_deep(height, eastward, northward, valid_rows)
    ensemble = jnp.stack([height, eastward, northward])
    obs_weight = obs_mask.astype(jnp.float32) * obs_precision
    observed = jnp.stack([obs_value, obs_weight])
    cell_total = float(
        members * row_count * col_count * lax.axis_size(MEMBER) * lax.axis_size(BAND)
    )
    root_scale = jnp.sqrt(jnp.float32(members - 1))
    increment = analyse_tiles(ensemble, observed, step_sizes, cell_total, root_scale, members)
    analysis = ensemble + increment[:, None]
    return (analysis[0], analysis[1], analysis[2])


def solution(mesh):
    torus = Mesh(
        mesh.devices.reshape(2, 4, 2, 4, 2),
        ("member_0", "member_1", "member_2", "band_0", "band_1"),
    )
    in_specs = (
        P(None, MEMBER, BAND),
        P(None, MEMBER, BAND),
        P(None, MEMBER, BAND),
        P(MEMBER, BAND),
        P(MEMBER, BAND),
        P(MEMBER, BAND),
        P(),
    )
    out_specs = (P(None, MEMBER, BAND), P(None, MEMBER, BAND), P(None, MEMBER, BAND))
    return jax.shard_map(
        per_device, mesh=torus, in_specs=in_specs, out_specs=out_specs, check_vma=False
    )
```

profile of v0, /device:TPU:2, one launch (start us, length us, event | category | flops | bytes accessed | tf_op | source)
XLA Modules:
  0.0 401.4 jit_solution(12849979625109068279)
XLA Ops:
  0.7 2.5 pad_maximum_fusion.15
  6.2 3.4 collective-permute-done.1
  9.7 2.1 pad_maximum_fusion.3
  11.8 5.3 %fusion.117 = (f32[3,80,36,2]{3,2,1,0:T(8,128)}, f32[3,80,36,2]{3,2,1,0:T(8,128)}) fusion(f32[3,80,36,128]{3,2,1,0:T(8,128)S(1)} %pad_maximum_fusion.3), kind=kLoop, calls=%fused_computation.180 | loop fusion | bytes 276480 | tf_op jit(solution)/shard_map/slice | solution.py:25
  17.1 3.8 copy.10
  20.9 3.9 collective-permute-start.2
  24.9 3.8 copy.11
  30.4 3.6 copy.12
  35.5 3.5 copy.13
  39.0 10.7 %pad_maximum_fusion = f32[3,80,36,132]{3,2,1,0:T(8,128)S(1)} fusion(f32[3,80,36,2]{3,2,1,0:T(8,128)} %copy.13, f32[3,80,2,128]{3,2,1,0:T(2,128)S(1)} %collective-permute-done.1, f32[1,80,32,128]{3,2,1,0:T(8,128)S(1)} %bitcast.125, f32[1,80,32,128]{3,2,1,0:T(8,128)S(1)} %bitcast.128, f32[1,80,32,128]{3,2,1,0:T(8,128)} %bitcast.131, ...), kind=kLoop, calls=%fused_computation | loop fusion | flops 6842880 | bytes 9123840 | tf_op jit(solution)/shard_map/concatenate | solution.py:28
  49.7 2.3 slice_bitcast_fusion.8
  52.0 5.8 %fusion.23 = f32[80,34,130]{2,1,0:T(8,128)S(1)} fusion(f32[80,36,132]{2,1,0:T(8,128)S(1)} %get-tuple-element.10, f32[80,36,132]{2,1,0:T(8,128)S(1)} %get-tuple-element.11, f32[80,36,132]{2,1,0:T(8,128)} %get-tuple-element.9, pred[34]{0:T(512)(128)(4,1)S(1)} %copy-done.24), kind=kLoop, calls=%fused_computation.44 | loop fusion | flops 2121600 | bytes 8486434 | tf_op jit(solution)/shard_map/jit(_where)/select_n | solution.py:75
  59.5 5.1 %collective-permute-start.4 = (f32[3,80,2,128]{3,2,1,0:T(2,128)S(1)}, f32[3,80,2,128]{3,2,1,0:T(2,128)S(1)}, u32[]{:S(2)}, u32[]{:S(2)}) collective-permute-start(f32[3,80,2,128]{3,2,1,0:T(2,128)S(1)} %get-tuple-element.29), channel_id=1, source_target_pairs={{0,8},{8,16},{16,24},{24,32},{32,40},{40,48},{48,56},{56,64},{64,7... | collective-permute-start | bytes 737288 | tf_op jit(solution)/shard_map/ppermute | solution.py:24
  66.1 3.3 collective-permute-done.5
  70.4 5.3 %fusion.116 = (f32[3,80,36,2]{3,2,1,0:T(8,128)}, f32[3,80,36,2]{3,2,1,0:T(8,128)}) fusion(f32[3,80,36,128]{3,2,1,0:T(8,128)S(1)} %pad_maximum_fusion.4), kind=kLoop, calls=%fused_computation.179 | loop fusion | bytes 276480 | tf_op jit(solution)/shard_map/slice | solution.py:25
  75.7 3.8 copy.14
  81.1 3.8 copy.15
  84.9 3.0 collective-permute-start.7
  87.9 3.6 copy.16
  91.6 3.5 copy.17
  95.1 10.7 %pad_maximum_fusion.1 = f32[3,80,36,132]{3,2,1,0:T(8,128)S(1)} fusion(f32[3,80,36,2]{3,2,1,0:T(8,128)} %copy.17, f32[3,80,2,128]{3,2,1,0:T(2,128)S(1)} %collective-permute-done.5, f32[1,80,32,128]{3,2,1,0:T(8,128)S(1)} %bitcast.122, f32[1,80,32,128]{3,2,1,0:T(8,128)S(1)} %bitcast.119, f32[1,80,32,128]{3,2,1,0:T(8,128)} %copy-done.18, ...), kind=kLoop, calls=%fused_computation.1 | loop fusion | flops 6842880 | bytes 9123840 | tf_op jit(solution)/shard_map/concatenate | solution.py:28
  105.8 2.3 slice_bitcast_fusion.5
  108.1 5.8 %fusion.19 = f32[80,34,130]{2,1,0:T(8,128)S(1)} fusion(f32[80,36,132]{2,1,0:T(8,128)S(1)} %get-tuple-element.7, f32[80,36,132]{2,1,0:T(8,128)S(1)} %get-tuple-element.8, f32[80,36,132]{2,1,0:T(8,128)} %get-tuple-element.6, pred[34]{0:T(512)(128)(4,1)S(1)} %copy-done.25), kind=kLoop, calls=%fused_computation.35 | loop fusion | flops 2121600 | bytes 8486434 | tf_op jit(solution)/shard_map/jit(_where)/select_n | solution.py:75
  115.6 5.9 %collective-permute-start.8 = (f32[3,80,2,128]{3,2,1,0:T(2,128)S(1)}, f32[3,80,2,128]{3,2,1,0:T(2,128)S(1)}, u32[]{:S(2)}, u32[]{:S(2)}) collective-permute-start(f32[3,80,2,128]{3,2,1,0:T(2,128)S(1)} %get-tuple-element.27), channel_id=1, source_target_pairs={{0,8},{8,16},{16,24},{24,32},{32,40},{40,48},{48,56},{56,64},{64,7... | collective-permute-start | bytes 737288 | tf_op jit(solution)/shard_map/ppermute | solution.py:24
  125.9 5.3 %fusion.115 = (f32[3,80,36,2]{3,2,1,0:T(8,128)}, f32[3,80,36,2]{3,2,1,0:T(8,128)}) fusion(f32[3,80,36,128]{3,2,1,0:T(8,128)S(1)} %pad_maximum_fusion.5), kind=kLoop, calls=%fused_computation.178 | loop fusion | bytes 276480 | tf_op jit(solution)/shard_map/slice | solution.py:25
  131.2 3.8 copy.18
  135.1 3.9 collective-permute-start.10
  139.0 3.8 copy.19
  143.5 3.6 copy.20
  147.0 2.1 collective-permute-done.11
  149.1 3.5 copy.21
  152.6 10.7 %pad_maximum_fusion.2 = f32[3,80,36,132]{3,2,1,0:T(8,128)S(1)} fusion(f32[3,80,36,2]{3,2,1,0:T(8,128)} %copy.21, f32[3,80,2,128]{3,2,1,0:T(2,128)S(1)} %collective-permute-done.9, f32[1,80,32,128]{3,2,1,0:T(8,128)S(1)} %bitcast.116, f32[1,80,32,128]{3,2,1,0:T(8,128)S(1)} %bitcast.113, f32[1,80,32,128]{3,2,1,0:T(8,128)} %copy-done.17, ...), kind=kLoop, calls=%fused_computation.2 | loop fusion | flops 6842880 | bytes 9123840 | tf_op jit(solution)/shard_map/concatenate | solution.py:28
  163.4 2.3 slice_bitcast_fusion.2
  165.7 5.6 %fusion.15 = f32[80,34,130]{2,1,0:T(8,128)S(1)} fusion(f32[80,36,132]{2,1,0:T(8,128)S(1)} %get-tuple-element.4, f32[80,36,132]{2,1,0:T(8,128)S(1)} %get-tuple-element.5, f32[80,36,132]{2,1,0:T(8,128)} %get-tuple-element.3, pred[34]{0:T(512)(128)(4,1)S(1)} %copy-done.26), kind=kLoop, calls=%fused_computation.26 | loop fusion | flops 2121600 | bytes 8486434 | tf_op jit(solution)/shard_map/jit(_where)/select_n | solution.py:75
  175.8 5.2 %collective-permute-start.12 = (f32[80,32,128]{2,1,0:T(8,128)S(1)}, f32[80,32,128]{2,1,0:T(8,128)S(1)}, u32[]{:S(2)}, u32[]{:S(2)}) collective-permute-start(f32[80,32,128]{2,1,0:T(8,128)S(1)} %add_multiply_fusion.1), channel_id=1, source_target_pairs={{0,8},{8,16},{16,24},{24,32},{32,40},{40,48},{48,56},{56,64},{64,7... | collective-permute-start | bytes 3932168 | tf_op jit(solution)/shard_map/ppermute | solution.py:24
  183.5 3.1 collective-permute-done.13
  186.6 2.3 fusion.39
  195.4 2.8 copy.23
  198.2 3.0 collective-permute-start.15
  201.2 23.3 %collective-permute-done.14 = f32[80,32,32]{0,2,1:T(8,128)} collective-permute-done((f32[80,32,32]{0,2,1:T(8,128)S(1)}, f32[80,32,32]{0,2,1:T(8,128)}, u32[]{:S(2)}, u32[]{:S(2)}) %collective-permute-start.14) | collective-permute-done | bytes 327712 | tf_op jit(solution)/shard_map/ppermute | solution.py:24
  224.5 3.0 copy.24
  227.6 3.0 copy.25
  230.6 6.4 %multiply_reduce_fusion.3 = (f32[]{:T(128)}, f32[80,32,128]{2,1,0:T(8,128)}) fusion(s32[192]{0:T(256)S(1)} %iota_add_fusion, f32[80,32,32]{2,1,0:T(8,128)} %copy.25, f32[80,32,128]{2,1,0:T(8,128)} %copy-done.20, f32[80,32,32]{2,1,0:T(8,128)} %copy.24), kind=kOutput, calls=%fused_computation.99 | convolution fusion | flops 757137408 | bytes 3277572 | tf_op jit(solution)/shard_map/mrjk,bk->mrjb/dot_general | solution.py:56
  237.1 14.6 %psum.70 = f32[]{:T(128)} all-reduce(f32[]{:T(128)} %get-tuple-element.46), channel_id=1, replica_groups=mesh['member_0'=2,'member_1'=4,'member_2'=2,'band_0'=4,'band_1'=2] {'mem..., use_global_device_ids=true, to_apply=%region_2.3 | all-reduce | flops 1 | bytes 8 | tf_op jit(solution)/shard_map/psum | solution.py:34
  251.6 9.2 %psum.71 = f32[]{:T(128)} all-reduce(f32[]{:T(128)} %psum.70), channel_id=1, replica_groups=mesh['member_0'=2,'member_1'=4,'member_2'=2,'band_0'=4,'band_1'=2] {'mem..., use_global_device_ids=true, to_apply=%region_3.4 | all-reduce | flops 1 | bytes 8 | tf_op jit(solution)/shard_map/psum | solution.py:34
  261.4 5.0 %psum.72 = f32[]{:T(128)} all-reduce(f32[]{:T(128)} %psum.71), channel_id=1, replica_groups=mesh['member_0'=2,'member_1'=4,'member_2'=2,'band_0'=4,'band_1'=2] {'mem..., use_global_device_ids=true, to_apply=%region_4.5 | all-reduce | flops 1 | bytes 8 | tf_op jit(solution)/shard_map/psum | solution.py:34
  267.1 10.8 %psum.73 = f32[]{:T(128)} all-reduce(f32[]{:T(128)} %psum.72), channel_id=1, replica_groups=mesh['member_0'=2,'member_1'=4,'member_2'=2,'band_0'=4,'band_1'=2] {'ban..., use_global_device_ids=true, to_apply=%region_5.6 | all-reduce | flops 1 | bytes 8 | tf_op jit(solution)/shard_map/psum | solution.py:34
  277.9 7.2 %psum.74 = f32[]{:T(128)} all-reduce(f32[]{:T(128)} %psum.73), channel_id=1, replica_groups=mesh['member_0'=2,'member_1'=4,'member_2'=2,'band_0'=4,'band_1'=2] {'ban..., use_global_device_ids=true, to_apply=%region_6.7 | all-reduce | flops 1 | bytes 8 | tf_op jit(solution)/shard_map/psum | solution.py:34
  294.0 2.7 collective-permute-done.17
  296.7 2.3 fusion.36
  304.0 3.6 collective-permute-start.18
  307.6 2.8 copy.27
  310.4 2.7 collective-permute-start.19
  313.1 7.0 %collective-permute-done.18 = f32[80,32,32]{0,2,1:T(8,128)} collective-permute-done((f32[80,32,32]{0,2,1:T(8,128)S(1)}, f32[80,32,32]{0,2,1:T(8,128)}, u32[]{:S(2)}, u32[]{:S(2)}) %collective-permute-start.18) | collective-permute-done | bytes 327712 | tf_op jit(solution)/shard_map/ppermute | solution.py:24
  320.0 3.0 copy.28
  324.2 3.0 copy.29
  327.2 6.8 %multiply_reduce_fusion.2 = (f32[]{:T(128)}, f32[80,32,128]{2,1,0:T(8,128)}) fusion(s32[192]{0:T(256)S(1)} %iota_add_fusion, f32[80,32,32]{2,1,0:T(8,128)} %copy.29, f32[80,32,128]{2,1,0:T(8,128)} %copy-done.19, f32[80,32,32]{2,1,0:T(8,128)} %copy.28, f32[80,32,128]{2,1,0:T(8,128)} %get-tuple-element.47, f32[]{:T(128)S(6)} %div.55), kind=kOutput, calls=%fused_computation.96 | convolution fusion | flops 757792768 | bytes 4588296 | tf_op jit(solution)/shard_map/mrjk,bk->mrjb/dot_general | solution.py:56
  334.0 28.9 %psum.75 = f32[]{:T(128)} all-reduce(f32[]{:T(128)} %get-tuple-element.48), channel_id=1, replica_groups=mesh['member_0'=2,'member_1'=4,'member_2'=2,'band_0'=4,'band_1'=2] {'mem..., use_global_device_ids=true, to_apply=%region_9.10 | all-reduce | flops 1 | bytes 8 | tf_op jit(solution)/shard_map/psum | solution.py:34
  363.0 9.3 %psum.76 = f32[]{:T(128)} all-reduce(f32[]{:T(128)} %psum.75), channel_id=1, replica_groups=mesh['member_0'=2,'member_1'=4,'member_2'=2,'band_0'=4,'band_1'=2] {'mem..., use_global_device_ids=true, to_apply=%region_10.11 | all-reduce | flops 1 | bytes 8 | tf_op jit(solution)/shard_map/psum | solution.py:34
  372.3 3.1 psum.77
  376.1 11.4 %psum.78 = f32[]{:T(128)} all-reduce(f32[]{:T(128)} %psum.77), channel_id=1, replica_groups=mesh['member_0'=2,'member_1'=4,'member_2'=2,'band_0'=4,'band_1'=2] {'ban..., use_global_device_ids=true, to_apply=%region_12.13 | all-reduce | flops 1 | bytes 8 | tf_op jit(solution)/shard_map/psum | solution.py:34
  387.4 7.6 %psum.79 = f32[]{:T(128)} all-reduce(f32[]{:T(128)} %psum.78), channel_id=1, replica_groups=mesh['member_0'=2,'member_1'=4,'member_2'=2,'band_0'=4,'band_1'=2] {'ban..., use_global_device_ids=true, to_apply=%region_13.14 | all-reduce | flops 1 | bytes 8 | tf_op jit(solution)/shard_map/psum | solution.py:34
  395.7 2.1 subtract_multiply_fusion.1
  399.2 2.0 slice_bitcast_fusion.9
  (109 shorter events, 48.0 us)
Async XLA Ops:
  0.6 9.0 %copy-start.15 = (f32[80,32,128]{2,1,0:T(8,128)S(1)}, f32[80,32,128]{2,1,0:T(8,128)}, u32[]{:S(2)}) copy-start(f32[80,32,128]{2,1,0:T(8,128)} %param.8) | copy-start | bytes 3932164
  0.6 9.0 %copy-start.13 = (f32[80,32,128]{2,1,0:T(8,128)S(1)}, f32[80,32,128]{2,1,0:T(8,128)}, u32[]{:S(2)}) copy-start(f32[80,32,128]{2,1,0:T(8,128)} %param.9) | copy-start | bytes 3932164
  3.2 3.1 collective-permute-start
  4.9 4.8 %collective-permute-start.1 = (f32[3,80,2,128]{3,2,1,0:T(2,128)S(1)}, f32[3,80,2,128]{3,2,1,0:T(2,128)S(1)}, u32[]{:S(2)}, u32[]{:S(2)}) collective-permute-start(f32[3,80,2,128]{3,2,1,0:T(2,128)S(1)} %get-tuple-element.32), channel_id=1, source_target_pairs={{8,0},{16,8},{24,16},{32,24},{40,32},{48,40},{56,48},{64,56},{72,6... | collective-permute-start | bytes 737288 | tf_op jit(solution)/shard_map/ppermute | solution.py:27
  20.9 9.5 %collective-permute-start.2 = (f32[3,80,36,2]{1,3,2,0:T(2,128)S(1)}, f32[3,80,36,2]{1,3,2,0:T(2,128)S(1)}, u32[]{:S(2)}, u32[]{:S(2)}) collective-permute-start(f32[3,80,36,2]{1,3,2,0:T(2,128)S(1)} %copy.10), channel_id=1, source_target_pairs={{0,1},{1,2},{2,3},{3,4},{4,5},{5,6},{6,7},{7,0},{8,9},{9,10},{10,1... | collective-permute-start | bytes 207368 | tf_op jit(solution)/shard_map/ppermute | solution.py:24
  28.7 6.8 %collective-permute-start.3 = (f32[3,80,36,2]{1,3,2,0:T(2,128)S(1)}, f32[3,80,36,2]{1,3,2,0:T(2,128)S(1)}, u32[]{:S(2)}, u32[]{:S(2)}) collective-permute-start(f32[3,80,36,2]{1,3,2,0:T(2,128)S(1)} %copy.11), channel_id=1, source_target_pairs={{1,0},{2,1},{3,2},{4,3},{5,4},{6,5},{7,6},{0,7},{9,8},{10,9},{11,1... | collective-permute-start | bytes 207368 | tf_op jit(solution)/shard_map/ppermute | solution.py:27
  49.7 2.3 copy-start.24
  52.0 5.9 %copy-start.14 = (f32[80,32,128]{2,1,0:T(8,128)S(1)}, f32[80,32,128]{2,1,0:T(8,128)}, u32[]{:S(2)}) copy-start(f32[80,32,128]{2,1,0:T(8,128)} %param.9) | copy-start | bytes 3932164
  52.0 5.9 %copy-start.16 = (f32[80,32,128]{2,1,0:T(8,128)S(1)}, f32[80,32,128]{2,1,0:T(8,128)}, u32[]{:S(2)}) copy-start(f32[80,32,128]{2,1,0:T(8,128)} %param.8) | copy-start | bytes 3932164
  59.3 16.4 %copy-start.18 = (f32[1,80,32,128]{3,2,1,0:T(8,128)}, f32[1,80,32,128]{3,2,1,0:T(8,128)S(1)}, u32[]{:S(2)}) copy-start(f32[1,80,32,128]{3,2,1,0:T(8,128)S(1)} %get-tuple-element.35) | copy-start | bytes 3932164
  59.3 35.7 %copy-start.9 = (f32[80,32,128]{2,1,0:T(8,128)}, f32[80,32,128]{2,1,0:T(8,128)S(1)}, u32[]{:S(2)}) copy-start(f32[80,32,128]{2,1,0:T(8,128)S(1)} %get-tuple-element.16) | copy-start | bytes 3932164
  59.3 35.7 %copy-start.11 = (f32[80,32,128]{2,1,0:T(8,128)}, f32[80,32,128]{2,1,0:T(8,128)S(1)}, u32[]{:S(2)}) copy-start(f32[80,32,128]{2,1,0:T(8,128)S(1)} %get-tuple-element.17) | copy-start | bytes 3932164
  59.5 6.6 %collective-permute-start.4 = (f32[3,80,2,128]{3,2,1,0:T(2,128)S(1)}, f32[3,80,2,128]{3,2,1,0:T(2,128)S(1)}, u32[]{:S(2)}, u32[]{:S(2)}) collective-permute-start(f32[3,80,2,128]{3,2,1,0:T(2,128)S(1)} %get-tuple-element.29), channel_id=1, source_target_pairs={{0,8},{8,16},{16,24},{24,32},{32,40},{40,48},{48,56},{56,64},{64,7... | collective-permute-start | bytes 737288 | tf_op jit(solution)/shard_map/ppermute | solution.py:24
  64.6 4.8 %collective-permute-start.5 = (f32[3,80,2,128]{3,2,1,0:T(2,128)S(1)}, f32[3,80,2,128]{3,2,1,0:T(2,128)S(1)}, u32[]{:S(2)}, u32[]{:S(2)}) collective-permute-start(f32[3,80,2,128]{3,2,1,0:T(2,128)S(1)} %get-tuple-element.30), channel_id=1, source_target_pairs={{8,0},{16,8},{24,16},{32,24},{40,32},{48,40},{56,48},{64,56},{72,6... | collective-permute-start | bytes 737288 | tf_op jit(solution)/shard_map/ppermute | solution.py:27
  79.5 8.4 %collective-permute-start.6 = (f32[3,80,36,2]{1,3,2,0:T(2,128)S(1)}, f32[3,80,36,2]{1,3,2,0:T(2,128)S(1)}, u32[]{:S(2)}, u32[]{:S(2)}) collective-permute-start(f32[3,80,36,2]{1,3,2,0:T(2,128)S(1)} %copy.14), channel_id=1, source_target_pairs={{0,1},{1,2},{2,3},{3,4},{4,5},{5,6},{6,7},{7,0},{8,9},{9,10},{10,1... | collective-permute-start | bytes 207368 | tf_op jit(solution)/shard_map/ppermute | solution.py:24
  84.9 6.7 %collective-permute-start.7 = (f32[3,80,36,2]{1,3,2,0:T(2,128)S(1)}, f32[3,80,36,2]{1,3,2,0:T(2,128)S(1)}, u32[]{:S(2)}, u32[]{:S(2)}) collective-permute-start(f32[3,80,36,2]{1,3,2,0:T(2,128)S(1)} %copy.15), channel_id=1, source_target_pairs={{1,0},{2,1},{3,2},{4,3},{5,4},{6,5},{7,6},{0,7},{9,8},{10,9},{11,1... | collective-permute-start | bytes 207368 | tf_op jit(solution)/shard_map/ppermute | solution.py:27
  105.8 2.3 copy-start.25
  108.1 5.9 %copy-start.10 = (f32[80,32,128]{2,1,0:T(8,128)S(1)}, f32[80,32,128]{2,1,0:T(8,128)}, u32[]{:S(2)}) copy-start(f32[80,32,128]{2,1,0:T(8,128)} %copy-done.9) | copy-start | bytes 3932164
  108.1 5.9 %copy-start.12 = (f32[80,32,128]{2,1,0:T(8,128)S(1)}, f32[80,32,128]{2,1,0:T(8,128)}, u32[]{:S(2)}) copy-start(f32[80,32,128]{2,1,0:T(8,128)} %copy-done.11) | copy-start | bytes 3932164
  115.4 15.8 %copy-start.17 = (f32[1,80,32,128]{3,2,1,0:T(8,128)}, f32[1,80,32,128]{3,2,1,0:T(8,128)S(1)}, u32[]{:S(2)}) copy-start(f32[1,80,32,128]{3,2,1,0:T(8,128)S(1)} %get-tuple-element.34) | copy-start | bytes 3932164
  115.4 37.2 %copy-start.5 = (f32[80,32,128]{2,1,0:T(8,128)}, f32[80,32,128]{2,1,0:T(8,128)S(1)}, u32[]{:S(2)}) copy-start(f32[80,32,128]{2,1,0:T(8,128)S(1)} %get-tuple-element.14) | copy-start | bytes 3932164
  115.4 37.2 %copy-start.7 = (f32[80,32,128]{2,1,0:T(8,128)}, f32[80,32,128]{2,1,0:T(8,128)S(1)}, u32[]{:S(2)}) copy-start(f32[80,32,128]{2,1,0:T(8,128)S(1)} %get-tuple-element.15) | copy-start | bytes 3932164
  115.6 7.6 %collective-permute-start.8 = (f32[3,80,2,128]{3,2,1,0:T(2,128)S(1)}, f32[3,80,2,128]{3,2,1,0:T(2,128)S(1)}, u32[]{:S(2)}, u32[]{:S(2)}) collective-permute-start(f32[3,80,2,128]{3,2,1,0:T(2,128)S(1)} %get-tuple-element.27), channel_id=1, source_target_pairs={{0,8},{8,16},{16,24},{24,32},{32,40},{40,48},{48,56},{56,64},{64,7... | collective-permute-start | bytes 737288 | tf_op jit(solution)/shard_map/ppermute | solution.py:24
  121.6 3.4 collective-permute-start.9
  135.1 8.4 %collective-permute-start.10 = (f32[3,80,36,2]{1,3,2,0:T(2,128)S(1)}, f32[3,80,36,2]{1,3,2,0:T(2,128)S(1)}, u32[]{:S(2)}, u32[]{:S(2)}) collective-permute-start(f32[3,80,36,2]{1,3,2,0:T(2,128)S(1)} %copy.18), channel_id=1, source_target_pairs={{0,1},{1,2},{2,3},{3,4},{4,5},{5,6},{6,7},{7,0},{8,9},{9,10},{10,1... | collective-permute-start | bytes 207368 | tf_op jit(solution)/shard_map/ppermute | solution.py:24
  142.8 6.3 %collective-permute-start.11 = (f32[3,80,36,2]{1,3,2,0:T(2,128)S(1)}, f32[3,80,36,2]{1,3,2,0:T(2,128)S(1)}, u32[]{:S(2)}, u32[]{:S(2)}) collective-permute-start(f32[3,80,36,2]{1,3,2,0:T(2,128)S(1)} %copy.19), channel_id=1, source_target_pairs={{1,0},{2,1},{3,2},{4,3},{5,4},{6,5},{7,6},{0,7},{9,8},{10,9},{11,1... | collective-permute-start | bytes 207368 | tf_op jit(solution)/shard_map/ppermute | solution.py:27
  163.3 2.3 copy-start.26
  165.7 5.7 %copy-start.6 = (f32[80,32,128]{2,1,0:T(8,128)S(1)}, f32[80,32,128]{2,1,0:T(8,128)}, u32[]{:S(2)}) copy-start(f32[80,32,128]{2,1,0:T(8,128)} %copy-done.5) | copy-start | bytes 3932164
  165.7 5.7 %copy-start.8 = (f32[80,32,128]{2,1,0:T(8,128)S(1)}, f32[80,32,128]{2,1,0:T(8,128)}, u32[]{:S(2)}) copy-start(f32[80,32,128]{2,1,0:T(8,128)} %copy-done.7) | copy-start | bytes 3932164
  172.8 1.2 copy-start
  173.1 0.9 copy-start.21
  173.1 0.9 copy-start.22
  173.1 0.9 copy-start.23
  174.0 1.9 copy-start.3
  175.8 7.7 %collective-permute-start.12 = (f32[80,32,128]{2,1,0:T(8,128)S(1)}, f32[80,32,128]{2,1,0:T(8,128)S(1)}, u32[]{:S(2)}, u32[]{:S(2)}) collective-permute-start(f32[80,32,128]{2,1,0:T(8,128)S(1)} %add_multiply_fusion.1), channel_id=1, source_target_pairs={{0,8},{8,16},{16,24},{24,32},{32,40},{40,48},{48,56},{56,64},{64,7... | collective-permute-start | bytes 3932168 | tf_op jit(solution)/shard_map/ppermute | solution.py:24
  181.0 5.6 %collective-permute-start.13 = (f32[80,32,128]{2,1,0:T(8,128)S(1)}, f32[80,32,128]{2,1,0:T(8,128)S(1)}, u32[]{:S(2)}, u32[]{:S(2)}) collective-permute-start(f32[80,32,128]{2,1,0:T(8,128)S(1)} %add_multiply_fusion.1), channel_id=1, source_target_pairs={{8,0},{16,8},{24,16},{32,24},{40,32},{48,40},{56,48},{64,56},{72,6... | collective-permute-start | bytes 3932168 | tf_op jit(solution)/shard_map/ppermute | solution.py:27
  189.0 1.1 copy-start.20
  194.0 30.6 %collective-permute-start.14 = (f32[80,32,32]{0,2,1:T(8,128)S(1)}, f32[80,32,32]{0,2,1:T(8,128)}, u32[]{:S(2)}, u32[]{:S(2)}) collective-permute-start(f32[80,32,32]{0,2,1:T(8,128)S(1)} %copy.22), channel_id=1, source_target_pairs={{0,1},{1,2},{2,3},{3,4},{4,5},{5,6},{6,7},{7,0},{8,9},{9,10},{10,1... | collective-permute-start | bytes 983048 | tf_op jit(solution)/shard_map/ppermute | solution.py:24
  198.2 29.4 %collective-permute-start.15 = (f32[80,32,32]{0,2,1:T(8,128)}, f32[80,32,32]{0,2,1:T(8,128)}, u32[]{:S(2)}, u32[]{:S(2)}) collective-permute-start(f32[80,32,32]{0,2,1:T(8,128)} %copy.23), channel_id=1, source_target_pairs={{1,0},{2,1},{3,2},{4,3},{5,4},{6,5},{7,6},{0,7},{9,8},{10,9},{11,1... | collective-permute-start | bytes 983048 | tf_op jit(solution)/shard_map/ppermute | solution.py:27
  230.6 30.2 %copy-start.27 = (s32[2]{0:T(128)S(1)}, s32[2]{0:T(128)}, u32[]{:S(2)}) copy-start(s32[2]{0:T(128)} %param.13) | copy-start | bytes 28
  285.7 1.7 copy-start.1
  287.4 2.1 copy-start.4
  290.0 3.9 collective-permute-start.16
  291.4 5.3 %collective-permute-start.17 = (f32[80,32,128]{2,1,0:T(8,128)S(1)}, f32[80,32,128]{2,1,0:T(8,128)S(1)}, u32[]{:S(2)}, u32[]{:S(2)}) collective-permute-start(f32[80,32,128]{2,1,0:T(8,128)S(1)} %add_multiply_fusion), channel_id=1, source_target_pairs={{8,0},{16,8},{24,16},{32,24},{40,32},{48,40},{56,48},{64,56},{72,6... | collective-permute-start | bytes 3932168 | tf_op jit(solution)/shard_map/ppermute | solution.py:27
  299.0 1.1 copy-start.19
  304.0 16.0 %collective-permute-start.18 = (f32[80,32,32]{0,2,1:T(8,128)S(1)}, f32[80,32,32]{0,2,1:T(8,128)}, u32[]{:S(2)}, u32[]{:S(2)}) collective-permute-start(f32[80,32,32]{0,2,1:T(8,128)S(1)} %copy.26), channel_id=1, source_target_pairs={{0,1},{1,2},{2,3},{3,4},{4,5},{5,6},{6,7},{7,0},{8,9},{9,10},{10,1... | collective-permute-start | bytes 983048 | tf_op jit(solution)/shard_map/ppermute | solution.py:24
  310.4 13.8 %collective-permute-start.19 = (f32[80,32,32]{0,2,1:T(8,128)}, f32[80,32,32]{0,2,1:T(8,128)}, u32[]{:S(2)}, u32[]{:S(2)}) collective-permute-start(f32[80,32,32]{0,2,1:T(8,128)} %copy.27), channel_id=1, source_target_pairs={{1,0},{2,1},{3,2},{4,3},{5,4},{6,5},{7,6},{0,7},{9,8},{10,9},{11,1... | collective-permute-start | bytes 983048 | tf_op jit(solution)/shard_map/ppermute | solution.py:27
  395.7 2.1 copy-start.2
where the time goes:
time: 406 us; the launch traced here: 401 us
  blocking collectives  107 us (26%)
  local copies, waits for them, and re-layouts  101 us (25%)
  other arithmetic  68.6 us (17%)
  starting transfers between devices  51.6 us (13%)
  waiting for transfers between devices  51.5 us (13%)
  matrix products  17.9 us (4%)
  between operations  4.12 us (1%)
    psum x10, blocking collectives, one_axis_at_a_time(): array = lax.psum(array, axis)  107 us
    concatenate x6, other arithmetic, extended(): block = jnp.concatenate([low, block, high], axis=dim)  36.1 us
    slice x10, local copies, waits for them, and re-layouts, extended(): lax.slice_in_dim(block, block.shape[dim] - width, None, axis=dim)  35.3 us
    ppermute x10, starting transfers between devices, extended(): lax.ppermute(lax.slice_in_dim(block, block.shape[dim] - width, None, axis...  33.7 us
    ppermute x10, waiting for transfers between devices, extended(): lax.ppermute(lax.slice_in_dim(block, block.shape[dim] - width, None, axis...  32.4 us
    ppermute x10, waiting for transfers between devices, extended(): lax.ppermute(lax.slice_in_dim(block, 0, width, axis=dim), axis, backward)  19.1 us
    ppermute x10, starting transfers between devices, extended(): lax.ppermute(lax.slice_in_dim(block, 0, width, axis=dim), axis, backward)  17.9 us
    select_n x3, other arithmetic, advance_deep(): jnp.where(valid_rows[None, :, None], wide_height, jnp.zeros_like(wide_hei...  17.3 us
  transfers between devices with their start and end apart: 20, of which 13 were waited for; matrix products, arithmetic and copies ran while one was open for 9% of the time, Pallas kernels for 0%

commit v1 on v0

--- a/solution.py
+++ b/solution.py
@@ -31,7 +31,7 @@
 
 def one_axis_at_a_time(array, axes):
     for axis in axes:
-        array = lax.psum(array, axis)
+        array = jnp.sum(lax.all_gather(array, axis), axis=0)
     return array
 
 

time: 406 us -> 421 us (1.037)
  local copies, waits for them, and re-layouts: 101 us -> 118 us
  other arithmetic: 68.6 us -> 74.6 us
  blocking collectives: 107 us -> 101 us
    psum x10 -> x0, blocking collectives: 107 us -> none  [one_axis_at_a_time(): array = lax.psum(array, axis)]
    unnamed x0 -> x10, blocking collectives: none -> 101 us
    unnamed x56 -> x91, local copies, waits for them, and re-layouts: 5.32 us -> 22.1 us
    reduce_sum x0 -> x10, other arithmetic: none -> 6.03 us  [one_axis_at_a_time(): array = jnp.sum(lax.all_gather(array, axis), axis=0)]
where the time goes in v1:
time: 421 us; the launch traced here: 416 us
  local copies, waits for them, and re-layouts  118 us (28%)
  blocking collectives  101 us (24%)
  other arithmetic  74.6 us (18%)
  starting transfers between devices  51.4 us (12%)
  waiting for transfers between devices  49.8 us (12%)
  matrix products  18 us (4%)
    unnamed x10, blocking collectives  101 us
    concatenate x6, other arithmetic, extended(): block = jnp.concatenate([low, block, high], axis=dim)  36.1 us
    slice x10, local copies, waits for them, and re-layouts, extended(): lax.slice_in_dim(block, block.shape[dim] - width, None, axis=dim)  35.5 us
    ppermute x10, starting transfers between devices, extended(): lax.ppermute(lax.slice_in_dim(block, block.shape[dim] - width, None, axis...  33.7 us
    ppermute x10, waiting for transfers between devices, extended(): lax.ppermute(lax.slice_in_dim(block, block.shape[dim] - width, None, axis...  30.6 us
    unnamed x91, local copies, waits for them, and re-layouts  22.1 us
    ppermute x10, waiting for transfers between devices, extended(): lax.ppermute(lax.slice_in_dim(block, 0, width, axis=dim), axis, backward)  19.1 us
    ppermute x10, starting transfers between devices, extended(): lax.ppermute(lax.slice_in_dim(block, 0, width, axis=dim), axis, backward)  17.7 us
  transfers between devices with their start and end apart: 20, of which 13 were waited for; matrix products, arithmetic and copies ran while one was open for 9% of the time, Pallas kernels for 0%

profile of v1, /device:TPU:2, one launch (start us, length us, event | category | flops | bytes accessed | tf_op | source)
XLA Modules:
  0.0 416.2 jit_solution(14252123621898880435)
XLA Ops:
  0.7 2.5 pad_maximum_fusion.15
  6.2 3.4 collective-permute-done.1
  9.7 2.1 pad_maximum_fusion.3
  11.8 5.3 %fusion.117 = (f32[3,80,36,2]{3,2,1,0:T(8,128)}, f32[3,80,36,2]{3,2,1,0:T(8,128)}) fusion(f32[3,80,36,128]{3,2,1,0:T(8,128)S(1)} %pad_maximum_fusion.3), kind=kLoop, calls=%fused_computation.180 | loop fusion | bytes 276480 | tf_op jit(solution)/shard_map/slice | solution.py:25
  17.1 3.8 copy.10
  20.9 3.9 collective-permute-start.2
  24.9 3.8 copy.11
  30.3 3.6 copy.12
  35.5 3.5 copy.13
  39.0 10.7 %pad_maximum_fusion = f32[3,80,36,132]{3,2,1,0:T(8,128)S(1)} fusion(f32[3,80,36,2]{3,2,1,0:T(8,128)} %copy.13, f32[3,80,2,128]{3,2,1,0:T(2,128)S(1)} %collective-permute-done.1, f32[1,80,32,128]{3,2,1,0:T(8,128)S(1)} %bitcast.140, f32[1,80,32,128]{3,2,1,0:T(8,128)S(1)} %bitcast.143, f32[1,80,32,128]{3,2,1,0:T(8,128)} %bitcast.146, ...), kind=kLoop, calls=%fused_computation | loop fusion | flops 6842880 | bytes 9123840 | tf_op jit(solution)/shard_map/concatenate | solution.py:28
  49.7 2.3 slice_bitcast_fusion.8
  52.0 5.8 %fusion.23 = f32[80,34,130]{2,1,0:T(8,128)S(1)} fusion(f32[80,36,132]{2,1,0:T(8,128)S(1)} %get-tuple-element.10, f32[80,36,132]{2,1,0:T(8,128)S(1)} %get-tuple-element.11, f32[80,36,132]{2,1,0:T(8,128)} %get-tuple-element.9, pred[34]{0:T(512)(128)(4,1)S(1)} %copy-done.24), kind=kLoop, calls=%fused_computation.44 | loop fusion | flops 2121600 | bytes 8486434 | tf_op jit(solution)/shard_map/jit(_where)/select_n | solution.py:75
  59.5 5.1 %collective-permute-start.4 = (f32[3,80,2,128]{3,2,1,0:T(2,128)S(1)}, f32[3,80,2,128]{3,2,1,0:T(2,128)S(1)}, u32[]{:S(2)}, u32[]{:S(2)}) collective-permute-start(f32[3,80,2,128]{3,2,1,0:T(2,128)S(1)} %get-tuple-element.29), channel_id=1, source_target_pairs={{0,8},{8,16},{16,24},{24,32},{32,40},{40,48},{48,56},{56,64},{64,7... | collective-permute-start | bytes 737288 | tf_op jit(solution)/shard_map/ppermute | solution.py:24
  66.1 3.3 collective-permute-done.5
  70.4 5.3 %fusion.116 = (f32[3,80,36,2]{3,2,1,0:T(8,128)}, f32[3,80,36,2]{3,2,1,0:T(8,128)}) fusion(f32[3,80,36,128]{3,2,1,0:T(8,128)S(1)} %pad_maximum_fusion.4), kind=kLoop, calls=%fused_computation.179 | loop fusion | bytes 276480 | tf_op jit(solution)/shard_map/slice | solution.py:25
  75.7 3.8 copy.14
  81.1 3.8 copy.15
  85.0 3.0 collective-permute-start.7
  88.0 3.6 copy.16
  91.6 3.5 copy.17
  95.1 10.7 %pad_maximum_fusion.1 = f32[3,80,36,132]{3,2,1,0:T(8,128)S(1)} fusion(f32[3,80,36,2]{3,2,1,0:T(8,128)} %copy.17, f32[3,80,2,128]{3,2,1,0:T(2,128)S(1)} %collective-permute-done.5, f32[1,80,32,128]{3,2,1,0:T(8,128)S(1)} %bitcast.137, f32[1,80,32,128]{3,2,1,0:T(8,128)S(1)} %bitcast.134, f32[1,80,32,128]{3,2,1,0:T(8,128)} %copy-done.18, ...), kind=kLoop, calls=%fused_computation.1 | loop fusion | flops 6842880 | bytes 9123840 | tf_op jit(solution)/shard_map/concatenate | solution.py:28
  105.8 2.3 slice_bitcast_fusion.5
  108.1 5.8 %fusion.19 = f32[80,34,130]{2,1,0:T(8,128)S(1)} fusion(f32[80,36,132]{2,1,0:T(8,128)S(1)} %get-tuple-element.7, f32[80,36,132]{2,1,0:T(8,128)S(1)} %get-tuple-element.8, f32[80,36,132]{2,1,0:T(8,128)} %get-tuple-element.6, pred[34]{0:T(512)(128)(4,1)S(1)} %copy-done.25), kind=kLoop, calls=%fused_computation.35 | loop fusion | flops 2121600 | bytes 8486434 | tf_op jit(solution)/shard_map/jit(_where)/select_n | solution.py:75
  115.7 5.9 %collective-permute-start.8 = (f32[3,80,2,128]{3,2,1,0:T(2,128)S(1)}, f32[3,80,2,128]{3,2,1,0:T(2,128)S(1)}, u32[]{:S(2)}, u32[]{:S(2)}) collective-permute-start(f32[3,80,2,128]{3,2,1,0:T(2,128)S(1)} %get-tuple-element.27), channel_id=1, source_target_pairs={{0,8},{8,16},{16,24},{24,32},{32,40},{40,48},{48,56},{56,64},{64,7... | collective-permute-start | bytes 737288 | tf_op jit(solution)/shard_map/ppermute | solution.py:24
  125.9 5.3 %fusion.115 = (f32[3,80,36,2]{3,2,1,0:T(8,128)}, f32[3,80,36,2]{3,2,1,0:T(8,128)}) fusion(f32[3,80,36,128]{3,2,1,0:T(8,128)S(1)} %pad_maximum_fusion.5), kind=kLoop, calls=%fused_computation.178 | loop fusion | bytes 276480 | tf_op jit(solution)/shard_map/slice | solution.py:25
  131.3 3.8 copy.18
  135.1 3.9 collective-permute-start.10
  139.0 3.8 copy.19
  143.5 3.6 copy.20
  147.1 2.1 collective-permute-done.11
  149.2 3.5 copy.21
  152.7 10.7 %pad_maximum_fusion.2 = f32[3,80,36,132]{3,2,1,0:T(8,128)S(1)} fusion(f32[3,80,36,2]{3,2,1,0:T(8,128)} %copy.21, f32[3,80,2,128]{3,2,1,0:T(2,128)S(1)} %collective-permute-done.9, f32[1,80,32,128]{3,2,1,0:T(8,128)S(1)} %bitcast.131, f32[1,80,32,128]{3,2,1,0:T(8,128)S(1)} %bitcast.128, f32[1,80,32,128]{3,2,1,0:T(8,128)} %copy-done.17, ...), kind=kLoop, calls=%fused_computation.2 | loop fusion | flops 6842880 | bytes 9123840 | tf_op jit(solution)/shard_map/concatenate | solution.py:28
  163.4 2.3 slice_bitcast_fusion.2
  165.7 5.6 %fusion.15 = f32[80,34,130]{2,1,0:T(8,128)S(1)} fusion(f32[80,36,132]{2,1,0:T(8,128)S(1)} %get-tuple-element.4, f32[80,36,132]{2,1,0:T(8,128)S(1)} %get-tuple-element.5, f32[80,36,132]{2,1,0:T(8,128)} %get-tuple-element.3, pred[34]{0:T(512)(128)(4,1)S(1)} %copy-done.26), kind=kLoop, calls=%fused_computation.26 | loop fusion | flops 2121600 | bytes 8486434 | tf_op jit(solution)/shard_map/jit(_where)/select_n | solution.py:75
  175.9 5.2 %collective-permute-start.12 = (f32[80,32,128]{2,1,0:T(8,128)S(1)}, f32[80,32,128]{2,1,0:T(8,128)S(1)}, u32[]{:S(2)}, u32[]{:S(2)}) collective-permute-start(f32[80,32,128]{2,1,0:T(8,128)S(1)} %add_multiply_fusion.1), channel_id=1, source_target_pairs={{0,8},{8,16},{16,24},{24,32},{32,40},{40,48},{48,56},{56,64},{64,7... | collective-permute-start | bytes 3932168 | tf_op jit(solution)/shard_map/ppermute | solution.py:24
  183.6 3.1 collective-permute-done.13
  186.7 2.3 fusion.39
  192.0 2.0 copy.22
  195.5 2.8 copy.23
  198.3 3.0 collective-permute-start.15
  203.2 21.4 %collective-permute-done.14 = f32[80,32,32]{0,2,1:T(8,128)} collective-permute-done((f32[80,32,32]{0,2,1:T(8,128)S(1)}, f32[80,32,32]{0,2,1:T(8,128)}, u32[]{:S(2)}, u32[]{:S(2)}) %collective-permute-start.14) | collective-permute-done | bytes 327712 | tf_op jit(solution)/shard_map/ppermute | solution.py:24
  224.5 3.0 copy.24
  227.6 3.0 copy.25
  230.6 6.5 %multiply_reduce_fusion.3 = (f32[]{:T(128)}, f32[80,32,128]{2,1,0:T(8,128)}) fusion(s32[192]{0:T(256)S(1)} %iota_add_fusion, f32[80,32,32]{2,1,0:T(8,128)} %copy.25, f32[80,32,128]{2,1,0:T(8,128)} %copy-done.19, f32[80,32,32]{2,1,0:T(8,128)} %copy.24), kind=kOutput, calls=%fused_computation.99 | convolution fusion | flops 757137408 | bytes 3277572 | tf_op jit(solution)/shard_map/mrjk,bk->mrjb/dot_general | solution.py:56
  239.0 13.9 %all-reduce = f32[2]{0:T(128)S(1)} all-reduce(f32[2]{0:T(128)S(1)} %dynamic-update-slice), channel_id=1, replica_groups=mesh['member_0'=2,'member_1'=4,'member_2'=2,'band_0'=4,'band_1'=2] {'mem..., use_global_device_ids=true, to_apply=%add | all-reduce | flops 2 | bytes 16
  255.6 8.7 %all-reduce.1 = f32[4]{0:T(128)S(1)} all-reduce(f32[4]{0:T(128)S(1)} %dynamic-update-slice.1), channel_id=1, replica_groups=mesh['member_0'=2,'member_1'=4,'member_2'=2,'band_0'=4,'band_1'=2] {'mem..., use_global_device_ids=true, to_apply=%add.1 | all-reduce | flops 4 | bytes 32
  266.8 4.3 %all-reduce.2 = f32[2]{0:T(128)S(1)} all-reduce(f32[2]{0:T(128)S(1)} %dynamic-update-slice.2), channel_id=1, replica_groups=mesh['member_0'=2,'member_1'=4,'member_2'=2,'band_0'=4,'band_1'=2] {'mem..., use_global_device_ids=true, to_apply=%add.2 | all-reduce | flops 2 | bytes 16
  273.7 10.1 %all-reduce.3 = f32[4]{0:T(128)S(1)} all-reduce(f32[4]{0:T(128)S(1)} %dynamic-update-slice.3), channel_id=1, replica_groups=mesh['member_0'=2,'member_1'=4,'member_2'=2,'band_0'=4,'band_1'=2] {'ban..., use_global_device_ids=true, to_apply=%add.3 | all-reduce | flops 4 | bytes 32
  285.8 6.7 %all-reduce.4 = f32[2]{0:T(128)S(1)} all-reduce(f32[2]{0:T(128)S(1)} %dynamic-update-slice.4), channel_id=1, replica_groups=mesh['member_0'=2,'member_1'=4,'member_2'=2,'band_0'=4,'band_1'=2] {'ban..., use_global_device_ids=true, to_apply=%add.4 | all-reduce | flops 2 | bytes 16
  302.1 2.7 collective-permute-done.17
  304.8 2.3 fusion.36
  312.1 3.6 collective-permute-start.18
  315.7 2.8 copy.27
  318.5 2.7 collective-permute-start.19
  321.2 6.9 %collective-permute-done.18 = f32[80,32,32]{0,2,1:T(8,128)} collective-permute-done((f32[80,32,32]{0,2,1:T(8,128)S(1)}, f32[80,32,32]{0,2,1:T(8,128)}, u32[]{:S(2)}, u32[]{:S(2)}) %collective-permute-start.18) | collective-permute-done | bytes 327712 | tf_op jit(solution)/shard_map/ppermute | solution.py:24
  328.1 3.0 copy.28
  332.3 3.0 copy.29
  335.3 6.8 %multiply_reduce_fusion.2 = (f32[]{:T(128)}, f32[80,32,128]{2,1,0:T(8,128)}) fusion(s32[192]{0:T(256)S(1)} %iota_add_fusion, f32[80,32,32]{2,1,0:T(8,128)} %copy.29, f32[80,32,128]{2,1,0:T(8,128)} %copy-done.20, f32[80,32,32]{2,1,0:T(8,128)} %copy.28, f32[80,32,128]{2,1,0:T(8,128)} %get-tuple-element.47, f32[]{:T(128)S(6)} %div.55), kind=kOutput, calls=%fused_computation.96 | convolution fusion | flops 757792768 | bytes 4588296 | tf_op jit(solution)/shard_map/mrjk,bk->mrjb/dot_general | solution.py:56
  343.5 28.3 %all-reduce.5 = f32[2]{0:T(128)S(1)} all-reduce(f32[2]{0:T(128)S(1)} %dynamic-update-slice.5), channel_id=1, replica_groups=mesh['member_0'=2,'member_1'=4,'member_2'=2,'band_0'=4,'band_1'=2] {'mem..., use_global_device_ids=true, to_apply=%add.5 | all-reduce | flops 2 | bytes 16
  373.8 8.7 %all-reduce.6 = f32[4]{0:T(128)S(1)} all-reduce(f32[4]{0:T(128)S(1)} %dynamic-update-slice.6), channel_id=1, replica_groups=mesh['member_0'=2,'member_1'=4,'member_2'=2,'band_0'=4,'band_1'=2] {'mem..., use_global_device_ids=true, to_apply=%add.6 | all-reduce | flops 4 | bytes 32
  384.5 2.4 all-reduce.7
  389.6 10.7 %all-reduce.8 = f32[4]{0:T(128)S(1)} all-reduce(f32[4]{0:T(128)S(1)} %dynamic-update-slice.8), channel_id=1, replica_groups=mesh['member_0'=2,'member_1'=4,'member_2'=2,'band_0'=4,'band_1'=2] {'ban..., use_global_device_ids=true, to_apply=%add.8 | all-reduce | flops 4 | bytes 32
  402.3 7.0 %all-reduce.9 = f32[2]{0:T(128)S(1)} all-reduce(f32[2]{0:T(128)S(1)} %dynamic-update-slice.9), channel_id=1, replica_groups=mesh['member_0'=2,'member_1'=4,'member_2'=2,'band_0'=4,'band_1'=2] {'ban..., use_global_device_ids=true, to_apply=%add.9 | all-reduce | flops 2 | bytes 16
  410.5 2.1 subtract_multiply_fusion.1
  (154 shorter events, 70.9 us)
Async XLA Ops:
  0.6 9.0 %copy-start.15 = (f32[80,32,128]{2,1,0:T(8,128)S(1)}, f32[80,32,128]{2,1,0:T(8,128)}, u32[]{:S(2)}) copy-start(f32[80,32,128]{2,1,0:T(8,128)} %param.8) | copy-start | bytes 3932164
  0.6 9.0 %copy-start.13 = (f32[80,32,128]{2,1,0:T(8,128)S(1)}, f32[80,32,128]{2,1,0:T(8,128)}, u32[]{:S(2)}) copy-start(f32[80,32,128]{2,1,0:T(8,128)} %param.9) | copy-start | bytes 3932164
  3.2 3.1 collective-permute-start
  4.9 4.8 %collective-permute-start.1 = (f32[3,80,2,128]{3,2,1,0:T(2,128)S(1)}, f32[3,80,2,128]{3,2,1,0:T(2,128)S(1)}, u32[]{:S(2)}, u32[]{:S(2)}) collective-permute-start(f32[3,80,2,128]{3,2,1,0:T(2,128)S(1)} %get-tuple-element.32), channel_id=1, source_target_pairs={{8,0},{16,8},{24,16},{32,24},{40,32},{48,40},{56,48},{64,56},{72,6... | collective-permute-start | bytes 737288 | tf_op jit(solution)/shard_map/ppermute | solution.py:27
  20.9 9.4 %collective-permute-start.2 = (f32[3,80,36,2]{1,3,2,0:T(2,128)S(1)}, f32[3,80,36,2]{1,3,2,0:T(2,128)S(1)}, u32[]{:S(2)}, u32[]{:S(2)}) collective-permute-start(f32[3,80,36,2]{1,3,2,0:T(2,128)S(1)} %copy.10), channel_id=1, source_target_pairs={{0,1},{1,2},{2,3},{3,4},{4,5},{5,6},{6,7},{7,0},{8,9},{9,10},{10,1... | collective-permute-start | bytes 207368 | tf_op jit(solution)/shard_map/ppermute | solution.py:24
  28.7 6.8 %collective-permute-start.3 = (f32[3,80,36,2]{1,3,2,0:T(2,128)S(1)}, f32[3,80,36,2]{1,3,2,0:T(2,128)S(1)}, u32[]{:S(2)}, u32[]{:S(2)}) collective-permute-start(f32[3,80,36,2]{1,3,2,0:T(2,128)S(1)} %copy.11), channel_id=1, source_target_pairs={{1,0},{2,1},{3,2},{4,3},{5,4},{6,5},{7,6},{0,7},{9,8},{10,9},{11,1... | collective-permute-start | bytes 207368 | tf_op jit(solution)/shard_map/ppermute | solution.py:27
  49.7 2.3 copy-start.24
  52.0 5.9 %copy-start.14 = (f32[80,32,128]{2,1,0:T(8,128)S(1)}, f32[80,32,128]{2,1,0:T(8,128)}, u32[]{:S(2)}) copy-start(f32[80,32,128]{2,1,0:T(8,128)} %param.9) | copy-start | bytes 3932164
  52.0 5.9 %copy-start.16 = (f32[80,32,128]{2,1,0:T(8,128)S(1)}, f32[80,32,128]{2,1,0:T(8,128)}, u32[]{:S(2)}) copy-start(f32[80,32,128]{2,1,0:T(8,128)} %param.8) | copy-start | bytes 3932164
  59.3 16.4 %copy-start.18 = (f32[1,80,32,128]{3,2,1,0:T(8,128)}, f32[1,80,32,128]{3,2,1,0:T(8,128)S(1)}, u32[]{:S(2)}) copy-start(f32[1,80,32,128]{3,2,1,0:T(8,128)S(1)} %get-tuple-element.35) | copy-start | bytes 3932164
  59.3 35.8 %copy-start.9 = (f32[80,32,128]{2,1,0:T(8,128)}, f32[80,32,128]{2,1,0:T(8,128)S(1)}, u32[]{:S(2)}) copy-start(f32[80,32,128]{2,1,0:T(8,128)S(1)} %get-tuple-element.16) | copy-start | bytes 3932164
  59.3 35.7 %copy-start.11 = (f32[80,32,128]{2,1,0:T(8,128)}, f32[80,32,128]{2,1,0:T(8,128)S(1)}, u32[]{:S(2)}) copy-start(f32[80,32,128]{2,1,0:T(8,128)S(1)} %get-tuple-element.17) | copy-start | bytes 3932164
  59.5 6.6 %collective-permute-start.4 = (f32[3,80,2,128]{3,2,1,0:T(2,128)S(1)}, f32[3,80,2,128]{3,2,1,0:T(2,128)S(1)}, u32[]{:S(2)}, u32[]{:S(2)}) collective-permute-start(f32[3,80,2,128]{3,2,1,0:T(2,128)S(1)} %get-tuple-element.29), channel_id=1, source_target_pairs={{0,8},{8,16},{16,24},{24,32},{32,40},{40,48},{48,56},{56,64},{64,7... | collective-permute-start | bytes 737288 | tf_op jit(solution)/shard_map/ppermute | solution.py:24
  64.6 4.8 %collective-permute-start.5 = (f32[3,80,2,128]{3,2,1,0:T(2,128)S(1)}, f32[3,80,2,128]{3,2,1,0:T(2,128)S(1)}, u32[]{:S(2)}, u32[]{:S(2)}) collective-permute-start(f32[3,80,2,128]{3,2,1,0:T(2,128)S(1)} %get-tuple-element.30), channel_id=1, source_target_pairs={{8,0},{16,8},{24,16},{32,24},{40,32},{48,40},{56,48},{64,56},{72,6... | collective-permute-start | bytes 737288 | tf_op jit(solution)/shard_map/ppermute | solution.py:27
  79.6 8.4 %collective-permute-start.6 = (f32[3,80,36,2]{1,3,2,0:T(2,128)S(1)}, f32[3,80,36,2]{1,3,2,0:T(2,128)S(1)}, u32[]{:S(2)}, u32[]{:S(2)}) collective-permute-start(f32[3,80,36,2]{1,3,2,0:T(2,128)S(1)} %copy.14), channel_id=1, source_target_pairs={{0,1},{1,2},{2,3},{3,4},{4,5},{5,6},{6,7},{7,0},{8,9},{9,10},{10,1... | collective-permute-start | bytes 207368 | tf_op jit(solution)/shard_map/ppermute | solution.py:24
  85.0 6.7 %collective-permute-start.7 = (f32[3,80,36,2]{1,3,2,0:T(2,128)S(1)}, f32[3,80,36,2]{1,3,2,0:T(2,128)S(1)}, u32[]{:S(2)}, u32[]{:S(2)}) collective-permute-start(f32[3,80,36,2]{1,3,2,0:T(2,128)S(1)} %copy.15), channel_id=1, source_target_pairs={{1,0},{2,1},{3,2},{4,3},{5,4},{6,5},{7,6},{0,7},{9,8},{10,9},{11,1... | collective-permute-start | bytes 207368 | tf_op jit(solution)/shard_map/ppermute | solution.py:27
  105.8 2.3 copy-start.25
  108.1 5.9 %copy-start.10 = (f32[80,32,128]{2,1,0:T(8,128)S(1)}, f32[80,32,128]{2,1,0:T(8,128)}, u32[]{:S(2)}) copy-start(f32[80,32,128]{2,1,0:T(8,128)} %copy-done.9) | copy-start | bytes 3932164
  108.1 5.9 %copy-start.12 = (f32[80,32,128]{2,1,0:T(8,128)S(1)}, f32[80,32,128]{2,1,0:T(8,128)}, u32[]{:S(2)}) copy-start(f32[80,32,128]{2,1,0:T(8,128)} %copy-done.11) | copy-start | bytes 3932164
  115.4 15.8 %copy-start.17 = (f32[1,80,32,128]{3,2,1,0:T(8,128)}, f32[1,80,32,128]{3,2,1,0:T(8,128)S(1)}, u32[]{:S(2)}) copy-start(f32[1,80,32,128]{3,2,1,0:T(8,128)S(1)} %get-tuple-element.34) | copy-start | bytes 3932164
  115.4 37.2 %copy-start.5 = (f32[80,32,128]{2,1,0:T(8,128)}, f32[80,32,128]{2,1,0:T(8,128)S(1)}, u32[]{:S(2)}) copy-start(f32[80,32,128]{2,1,0:T(8,128)S(1)} %get-tuple-element.14) | copy-start | bytes 3932164
  115.4 37.2 %copy-start.7 = (f32[80,32,128]{2,1,0:T(8,128)}, f32[80,32,128]{2,1,0:T(8,128)S(1)}, u32[]{:S(2)}) copy-start(f32[80,32,128]{2,1,0:T(8,128)S(1)} %get-tuple-element.15) | copy-start | bytes 3932164
  115.7 7.6 %collective-permute-start.8 = (f32[3,80,2,128]{3,2,1,0:T(2,128)S(1)}, f32[3,80,2,128]{3,2,1,0:T(2,128)S(1)}, u32[]{:S(2)}, u32[]{:S(2)}) collective-permute-start(f32[3,80,2,128]{3,2,1,0:T(2,128)S(1)} %get-tuple-element.27), channel_id=1, source_target_pairs={{0,8},{8,16},{16,24},{24,32},{32,40},{40,48},{48,56},{56,64},{64,7... | collective-permute-start | bytes 737288 | tf_op jit(solution)/shard_map/ppermute | solution.py:24
  121.6 3.4 collective-permute-start.9
  135.1 8.4 %collective-permute-start.10 = (f32[3,80,36,2]{1,3,2,0:T(2,128)S(1)}, f32[3,80,36,2]{1,3,2,0:T(2,128)S(1)}, u32[]{:S(2)}, u32[]{:S(2)}) collective-permute-start(f32[3,80,36,2]{1,3,2,0:T(2,128)S(1)} %copy.18), channel_id=1, source_target_pairs={{0,1},{1,2},{2,3},{3,4},{4,5},{5,6},{6,7},{7,0},{8,9},{9,10},{10,1... | collective-permute-start | bytes 207368 | tf_op jit(solution)/shard_map/ppermute | solution.py:24
  142.9 6.3 %collective-permute-start.11 = (f32[3,80,36,2]{1,3,2,0:T(2,128)S(1)}, f32[3,80,36,2]{1,3,2,0:T(2,128)S(1)}, u32[]{:S(2)}, u32[]{:S(2)}) collective-permute-start(f32[3,80,36,2]{1,3,2,0:T(2,128)S(1)} %copy.19), channel_id=1, source_target_pairs={{1,0},{2,1},{3,2},{4,3},{5,4},{6,5},{7,6},{0,7},{9,8},{10,9},{11,1... | collective-permute-start | bytes 207368 | tf_op jit(solution)/shard_map/ppermute | solution.py:27
  163.4 2.3 copy-start.26
  165.7 5.7 %copy-start.6 = (f32[80,32,128]{2,1,0:T(8,128)S(1)}, f32[80,32,128]{2,1,0:T(8,128)}, u32[]{:S(2)}) copy-start(f32[80,32,128]{2,1,0:T(8,128)} %copy-done.5) | copy-start | bytes 3932164
  165.7 5.7 %copy-start.8 = (f32[80,32,128]{2,1,0:T(8,128)S(1)}, f32[80,32,128]{2,1,0:T(8,128)}, u32[]{:S(2)}) copy-start(f32[80,32,128]{2,1,0:T(8,128)} %copy-done.7) | copy-start | bytes 3932164
  172.8 1.2 copy-start
  173.1 0.9 copy-start.21
  173.1 0.9 copy-start.22
  173.2 0.9 copy-start.23
  174.0 1.9 copy-start.3
  175.9 7.7 %collective-permute-start.12 = (f32[80,32,128]{2,1,0:T(8,128)S(1)}, f32[80,32,128]{2,1,0:T(8,128)S(1)}, u32[]{:S(2)}, u32[]{:S(2)}) collective-permute-start(f32[80,32,128]{2,1,0:T(8,128)S(1)} %add_multiply_fusion.1), channel_id=1, source_target_pairs={{0,8},{8,16},{16,24},{24,32},{32,40},{40,48},{48,56},{56,64},{64,7... | collective-permute-start | bytes 3932168 | tf_op jit(solution)/shard_map/ppermute | solution.py:24
  181.0 5.6 %collective-permute-start.13 = (f32[80,32,128]{2,1,0:T(8,128)S(1)}, f32[80,32,128]{2,1,0:T(8,128)S(1)}, u32[]{:S(2)}, u32[]{:S(2)}) collective-permute-start(f32[80,32,128]{2,1,0:T(8,128)S(1)} %add_multiply_fusion.1), channel_id=1, source_target_pairs={{8,0},{16,8},{24,16},{32,24},{40,32},{48,40},{56,48},{64,56},{72,6... | collective-permute-start | bytes 3932168 | tf_op jit(solution)/shard_map/ppermute | solution.py:27
  189.0 1.1 copy-start.19
  192.0 9.3 %copy-start.32 = (u32[128]{0:T(128)S(1)}, u32[128]{0:T(128)}, u32[]{:S(2)}) copy-start(u32[128]{0:T(128)} %constant.81) | copy-start | bytes 1540
  192.0 9.9 %copy-start.31 = (u32[128]{0:T(128)S(1)}, u32[128]{0:T(128)}, u32[]{:S(2)}) copy-start(u32[128]{0:T(128)} %constant.86) | copy-start | bytes 1540
  192.0 10.5 %copy-start.27 = (s32[2]{0:T(128)S(1)}, s32[2]{0:T(128)}, u32[]{:S(2)}) copy-start(s32[2]{0:T(128)} %param.13) | copy-start | bytes 28
  194.1 30.5 %collective-permute-start.14 = (f32[80,32,32]{0,2,1:T(8,128)S(1)}, f32[80,32,32]{0,2,1:T(8,128)}, u32[]{:S(2)}, u32[]{:S(2)}) collective-permute-start(f32[80,32,32]{0,2,1:T(8,128)S(1)} %copy.22), channel_id=1, source_target_pairs={{0,1},{1,2},{2,3},{3,4},{4,5},{5,6},{6,7},{7,0},{8,9},{9,10},{10,1... | collective-permute-start | bytes 983048 | tf_op jit(solution)/shard_map/ppermute | solution.py:24
  198.3 29.3 %collective-permute-start.15 = (f32[80,32,32]{0,2,1:T(8,128)}, f32[80,32,32]{0,2,1:T(8,128)}, u32[]{:S(2)}, u32[]{:S(2)}) collective-permute-start(f32[80,32,32]{0,2,1:T(8,128)} %copy.23), channel_id=1, source_target_pairs={{1,0},{2,1},{3,2},{4,3},{5,4},{6,5},{7,6},{0,7},{9,8},{10,9},{11,1... | collective-permute-start | bytes 983048 | tf_op jit(solution)/shard_map/ppermute | solution.py:27
  230.6 7.8 %copy-start.30 = (u32[128]{0:T(128)S(1)}, u32[128]{0:T(128)}, u32[]{:S(2)}) copy-start(u32[128]{0:T(128)} %constant.91) | copy-start | bytes 1540
  230.6 24.3 %copy-start.29 = (u32[128]{0:T(128)S(1)}, u32[128]{0:T(128)}, u32[]{:S(2)}) copy-start(u32[128]{0:T(128)} %constant.96) | copy-start | bytes 1540
  230.6 35.6 %copy-start.28 = (u32[128]{0:T(128)S(1)}, u32[128]{0:T(128)}, u32[]{:S(2)}) copy-start(u32[128]{0:T(128)} %constant.101) | copy-start | bytes 1540
  293.8 1.7 copy-start.1
  295.5 2.1 copy-start.4
  298.1 3.9 collective-permute-start.16
  299.5 5.3 %collective-permute-start.17 = (f32[80,32,128]{2,1,0:T(8,128)S(1)}, f32[80,32,128]{2,1,0:T(8,128)S(1)}, u32[]{:S(2)}, u32[]{:S(2)}) collective-permute-start(f32[80,32,128]{2,1,0:T(8,128)S(1)} %add_multiply_fusion), channel_id=1, source_target_pairs={{8,0},{16,8},{24,16},{32,24},{40,32},{48,40},{56,48},{64,56},{72,6... | collective-permute-start | bytes 3932168 | tf_op jit(solution)/shard_map/ppermute | solution.py:27
  307.2 1.1 copy-start.20
  312.1 16.0 %collective-permute-start.18 = (f32[80,32,32]{0,2,1:T(8,128)S(1)}, f32[80,32,32]{0,2,1:T(8,128)}, u32[]{:S(2)}, u32[]{:S(2)}) collective-permute-start(f32[80,32,32]{0,2,1:T(8,128)S(1)} %copy.26), channel_id=1, source_target_pairs={{0,1},{1,2},{2,3},{3,4},{4,5},{5,6},{6,7},{7,0},{8,9},{9,10},{10,1... | collective-permute-start | bytes 983048 | tf_op jit(solution)/shard_map/ppermute | solution.py:24
  318.5 13.8 %collective-permute-start.19 = (f32[80,32,32]{0,2,1:T(8,128)}, f32[80,32,32]{0,2,1:T(8,128)}, u32[]{:S(2)}, u32[]{:S(2)}) collective-permute-start(f32[80,32,32]{0,2,1:T(8,128)} %copy.27), channel_id=1, source_target_pairs={{1,0},{2,1},{3,2},{4,3},{5,4},{6,5},{7,6},{0,7},{9,8},{10,9},{11,1... | collective-permute-start | bytes 983048 | tf_op jit(solution)/shard_map/ppermute | solution.py:27
  410.5 2.1 copy-start.2
